TPU v7x, 256 devices: a whole 4x4x8 slice. The times are simulated.
256 devices in a mesh: mp: 4 (over z_lo, core), fsdp: 16 (over y, x), dp: 4 (over z_hi).
Axes of the slice: x: 4, y: 4, z: 8 (z_hi: 4, z_lo: 2; z = z_hi * 2 + z_lo), core: 2. Of those that a mesh axis runs over, the one named last changes fastest.
Arguments:
- gen_noise: float32 [4, 4096, 128], P('dp', 'fsdp'), may hold values from -6 to 6
- renoise: float32 [4, 4096, 128], P('dp', 'fsdp'), may hold values from -120 to 120
- gen_step: int32 [4], P('dp'), may hold values from 250 to 999
- renoise_step: int32 [4], P('dp'), may hold values from 20 to 979
- text_pooled: bfloat16 [4, 768], P('dp'), may hold values from -6 to 6
- embed: bfloat16 [3, 64, 3072], replicated, may hold values from -0.75 to 0.75
- mod_weight: bfloat16 [3, 1024, 6144], P(None, None, 'fsdp'), may hold values from -0.1875 to 0.1875
- proj_weight: bfloat16 [3, 3072, 3072], P(None, 'fsdp', 'mp'), may hold values from -0.109375 to 0.109375
- unembed: bfloat16 [3, 64, 3072], P(None, None, 'mp'), may hold values from -0.109375 to 0.109375
Outputs:
- gen_grad: float32 [3072, 3072], P('fsdp', 'mp')
- score_gap: float32 [4, 4096, 128], P('dp', 'fsdp')
All inputs are finite; a program needn't handle non-finite values. Where the computation divides by a largest or mean magnitude, that divisor is 1e-20 or more.
Results may differ from a plain program's by a relative error of at most 0.03.
Values may be sent and summed in bfloat16 or wider, within the bound.
A program may use at most 128 MiB of HBM per device.

v0:
```python
import math
import jax
import jax.numpy as jnp
from jax import lax
from jax.sharding import PartitionSpec as P

D = 3072
CH = 64
TEMB = 256
GUIDANCE = 3.5
EPS_NORM = 1e-06
EPS_GAP = 1e-05


def sinusoid(timesteps):
    half_size = TEMB // 2
    frequency = jnp.exp(-math.log(10000.0) * jnp.arange(half_size, dtype=jnp.float32) / half_size)
    angles = timesteps.astype(jnp.float32)[:, None] * frequency[None, :]
    return jnp.concatenate([jnp.cos(angles), jnp.sin(angles)], axis=1)


def condition(timesteps, pooled):
    joined = jnp.concatenate([sinusoid(timesteps), pooled.astype(jnp.float32)], axis=1)
    return jax.nn.silu(joined).astype(jnp.bfloat16)


def normalize(values):
    average = jnp.mean(values, axis=1, keepdims=True)
    centred = values - average
    variance = jnp.mean(centred * centred, axis=1, keepdims=True)
    return centred * lax.rsqrt(variance + EPS_NORM)


def modulate(normed, modulation):
    return (normed * (1.0 + modulation[D:]) + modulation[:D]).astype(jnp.bfloat16)


def unembed_part(residual_sum, out_weight):
    return lax.dot_general(
        residual_sum.astype(jnp.bfloat16),
        out_weight,
        (((1,), (1,)), ((), ())),
        preferred_element_type=jnp.float32,
    )


def row_product(hidden, weight_piece):
    return jnp.dot(hidden, weight_piece, preferred_element_type=jnp.float32)


def body(
    gen_noise, renoise, gen_step, renoise_step, text_pooled, embed, mod_weight, proj_weight, unembed
):
    quarter = proj_weight.shape[2]
    col_start = lax.axis_index("mp") * quarter
    blank_text = jnp.zeros_like(text_pooled)
    noisy_vec = condition(renoise_step, text_pooled)
    local_mod = jnp.concatenate(
        [
            jnp.dot(
                condition(gen_step, text_pooled), mod_weight[0], preferred_element_type=jnp.float32
            ),
            jnp.dot(noisy_vec, mod_weight[1], preferred_element_type=jnp.float32),
            jnp.dot(
                condition(renoise_step, blank_text),
                mod_weight[1],
                preferred_element_type=jnp.float32,
            ),
            jnp.dot(noisy_vec, mod_weight[2], preferred_element_type=jnp.float32),
        ],
        axis=0,
    )
    modulation = lax.all_gather(local_mod, "fsdp", axis=1, tiled=True)
    latent = gen_noise[0].reshape(-1, CH)
    latent_bf = latent.astype(jnp.bfloat16)
    token_rows = latent.shape[0]
    embedded = jnp.dot(latent_bf, embed[0], preferred_element_type=jnp.float32)
    gen_hidden = modulate(normalize(embedded), modulation[0])
    gen_part = row_product(gen_hidden, lax.all_gather(proj_weight[0], "fsdp", axis=0, tiled=True))
    gen_cols = lax.dynamic_slice_in_dim(embedded, col_start, quarter, 1)
    clean_part = unembed_part(gen_cols + gen_part, unembed[0]).reshape(-1, 2 * CH)
    clean_lat = lax.psum(clean_part, "mp")
    noise_level = renoise_step[0].astype(jnp.float32) / 1000.0
    noisy_lat = (1.0 - noise_level) * clean_lat + noise_level * renoise[0]
    noisy_bf = noisy_lat.reshape(-1, CH).astype(jnp.bfloat16)
    teacher_in = jnp.dot(noisy_bf, embed[1], preferred_element_type=jnp.float32)
    teacher_norm = normalize(teacher_in)
    cond_hidden = modulate(teacher_norm, modulation[1])
    blank_hidden = modulate(teacher_norm, modulation[2])
    fake_in = jnp.dot(noisy_bf, embed[2], preferred_element_type=jnp.float32)
    fake_hidden = modulate(normalize(fake_in), modulation[3])
    pieces = (
        lax.all_gather(proj_weight[1], "fsdp", axis=0, tiled=True),
        lax.all_gather(proj_weight[2], "fsdp", axis=0, tiled=True),
    )
    cond_part = row_product(cond_hidden, pieces[0])
    blank_part = row_product(blank_hidden, pieces[0])
    fake_part = row_product(fake_hidden, pieces[1])
    teacher_cols = lax.dynamic_slice_in_dim(teacher_in, col_start, quarter, 1)
    fake_cols = lax.dynamic_slice_in_dim(fake_in, col_start, quarter, 1)
    cond_out, blank_out, fake_out = (
        lax.psum(
            unembed_part(teacher_cols + cond_part, unembed[1])
            .reshape(-1, 2 * CH)
            .astype(jnp.bfloat16),
            "mp",
        ).astype(jnp.float32),
        lax.psum(
            unembed_part(teacher_cols + blank_part, unembed[1])
            .reshape(-1, 2 * CH)
            .astype(jnp.bfloat16),
            "mp",
        ).astype(jnp.float32),
        lax.psum(
            unembed_part(fake_cols + fake_part, unembed[2])
            .reshape(-1, 2 * CH)
            .astype(jnp.bfloat16),
            "mp",
        ).astype(jnp.float32),
    )
    real_pred = noisy_lat - noise_level * (blank_out + GUIDANCE * (cond_out - blank_out))
    fake_pred = noisy_lat - noise_level * fake_out
    seq_len = token_rows * lax.axis_size("fsdp")
    gap_total = lax.psum(jnp.sum(jnp.abs(clean_lat - real_pred)), "fsdp")
    gap_scale = gap_total / (seq_len * CH) + EPS_GAP
    score_gap = (fake_pred - real_pred) / gap_scale
    all_tokens = seq_len * lax.axis_size("dp")
    cotangent = (score_gap / math.sqrt(all_tokens)).astype(jnp.bfloat16).reshape(-1, CH)
    upstream = jnp.dot(cotangent, unembed[0], preferred_element_type=jnp.float32).astype(
        jnp.bfloat16
    )
    row_terms = lax.psum_scatter(
        lax.dot_general(
            gen_hidden, upstream, (((0,), (0,)), ((), ())), preferred_element_type=jnp.float32
        ).astype(jnp.bfloat16),
        "fsdp",
        scatter_dimension=0,
        tiled=True,
    )
    gen_grad = lax.psum(row_terms, "dp").astype(jnp.float32)
    return (gen_grad, score_gap[None])


def solution(mesh):
    return jax.shard_map(
        body,
        mesh=mesh,
        in_specs=(
            P("dp", "fsdp", None),
            P("dp", "fsdp", None),
            P("dp"),
            P("dp"),
            P("dp", None),
            P(),
            P(None, None, "fsdp"),
            P(None, "fsdp", "mp"),
            P(None, None, "mp"),
        ),
        out_specs=(P("fsdp", "mp"), P("dp", "fsdp", None)),
        check_vma=False,
    )
```

profile of v0, /device:TPU:2, one launch (start us, length us, event | category | flops | bytes accessed | tf_op | source)
XLA Modules:
  0.0 498.5 jit_solution(18427168380381059458)
XLA Ops:
  7.2 2.1 fusion.104
  9.4 0.9 convert_element_type.109
  10.3 0.1 convert_element_type.110
  11.8 0.7 convert_reduce_fusion
  12.6 1.3 fusion.49
  13.9 1.3 fusion.53
  15.2 1.3 fusion.51
  16.6 1.3 fusion.55
  18.0 23.6 %all_gather.12 = f32[4,6144]{1,0:T(4,128)S(1)} all-gather(f32[4,384]{1,0:T(4,128)S(1)} %pad_maximum_fusion), channel_id=1, replica_groups=mesh['mp'=4,'fsdp'=16,'dp'=4] {'fsdp'}, dimensions={1}, use_global_device_ids=true | all-gather | bytes 104448 | tf_op jit(solution)/shard_map/all_gather | solution.py:73
  41.7 2.1 fusion.105
  43.8 2.6 copy-done
  46.4 0.8 multiply_reduce_fusion.2
  47.2 0.1 slice_add_fusion.1
  47.3 25.2 %all-gather.7.cloned.1.call-done = bf16[1,3072,768]{2,1,0:T(8,128)(2,1)} async-done(((bf16[1,192,768]{2,1,0:T(8,128)(2,1)}), bf16[1,3072,768]{2,1,0:T(8,128)(2,1)}) %all-gather.7.cloned.1.call-update) | async-done | bytes 4718608 | tf_op jit(solution)/shard_map/all_gather | solution.py:79
  72.5 7.9 %fusion.38 = f32[512,64]{1,0:T(8,128)S(1)} fusion(f32[512,3072]{1,0:T(8,128)} %copy-done, s32[]{:T(128)S(6)} %select_n.2, bf16[1,3072,768]{2,1,0:T(8,128)(2,1)} %all-gather.7.cloned.1.call-done, bf16[3,64,768]{2,1,0:T(8,128)(2,1)S(1)} %copy-done.6, f32[3072]{0:T(1024)S(1)} %bitcast.103, f32[3072]{0:T(1024)S(1)} %bitcast.105, f32[512]{0:T(512)S(1)} %add_rsqrt_fusion.2, ...), kind=kOutput, calls=%fused_computation.36 | convolution fusion | flops 2474901504 | bytes 12840964 | tf_op jit(solution)/shard_map/dot_general | solution.py:39
  80.3 0.8 reshape.200
  81.2 0.7 all-gather.9.cloned.1.call-update
  81.9 0.5 all-gather.11.cloned.1.call-update
  82.4 0.2 all-reduce.9.cloned.1.call-start
  82.7 38.7 %all-reduce.5.cloned.1.call-done = f32[256,128]{1,0:T(8,128)} async-done(((f32[256,128]{1,0:T(8,128)}), f32[256,128]{1,0:T(8,128)}) %all-reduce.5.cloned.1.call-update) | async-done | bytes 131088 | tf_op jit(solution)/shard_map/psum | solution.py:82
  121.4 0.9 fusion.85
  122.3 0.1 convert_element_type.120
  122.4 1.0 fusion.106
  123.4 2.7 copy-done.2
  126.1 0.8 multiply_reduce_fusion.1
  126.9 56.7 %all-gather.9.cloned.1.call-done = bf16[1,3072,768]{2,1,0:T(8,128)(2,1)} async-done(((bf16[1,192,768]{2,1,0:T(8,128)(2,1)}), bf16[1,3072,768]{2,1,0:T(8,128)(2,1)}) %all-gather.9.cloned.1.call-update) | async-done | bytes 4718608 | tf_op jit(solution)/shard_map/all_gather | solution.py:94
  183.6 7.9 %fusion.46 = bf16[512,64]{0,1:T(8,128)(2,1)S(1)} fusion(f32[512,3072]{1,0:T(8,128)} %copy-done.2, s32[]{:T(128)S(6)} %select_n.2, bf16[1,3072,768]{2,1,0:T(8,128)(2,1)} %all-gather.9.cloned.1.call-done, f32[3072]{0:T(1024)S(1)} %bitcast.111, f32[3072]{0:T(1024)S(1)} %bitcast.112, f32[512]{0:T(512)S(1)} %add_rsqrt_fusion.1, ...), kind=kOutput, calls=%fused_computation.39 | convolution fusion | flops 2474934272 | bytes 12775428 | tf_op jit(solution)/shard_map/dot_general | solution.py:39
  191.5 0.1 copy.12
  191.6 0.8 convert_element_type.124
  192.4 1.0 fusion.107
  193.4 2.7 copy-done.1
  196.1 0.8 multiply_reduce_fusion
  196.8 48.7 %all-gather.11.cloned.1.call-done = bf16[1,3072,768]{2,1,0:T(8,128)(2,1)} async-done(((bf16[1,192,768]{2,1,0:T(8,128)(2,1)}), bf16[1,3072,768]{2,1,0:T(8,128)(2,1)}) %all-gather.11.cloned.1.call-update) | async-done | bytes 4718608 | tf_op jit(solution)/shard_map/all_gather | solution.py:93
  245.5 7.9 %fusion.40 = bf16[512,64]{0,1:T(8,128)(2,1)S(1)} fusion(f32[512,3072]{1,0:T(8,128)} %copy-done.1, s32[]{:T(128)S(6)} %select_n.2, bf16[1,3072,768]{2,1,0:T(8,128)(2,1)} %all-gather.11.cloned.1.call-done, f32[3072]{0:T(1024)S(1)} %bitcast.109, f32[3072]{0:T(1024)S(1)} %bitcast.110, f32[512]{0:T(512)S(1)} %add_rsqrt_fusion, ...), kind=kOutput, calls=%fused_computation.37 | convolution fusion | flops 2474934272 | bytes 12775428 | tf_op jit(solution)/shard_map/dot_general | solution.py:39
  253.4 0.1 copy.14
  253.5 0.8 convert_element_type.134
  254.3 7.9 %fusion.43 = bf16[512,64]{0,1:T(8,128)(2,1)S(1)} fusion(f32[512,3072]{1,0:T(8,128)} %copy-done.1, s32[]{:T(128)S(6)} %select_n.2, bf16[1,3072,768]{2,1,0:T(8,128)(2,1)} %all-gather.11.cloned.1.call-done, f32[3072]{0:T(1024)S(1)} %bitcast.108, f32[3072]{0:T(1024)S(1)} %bitcast.107, f32[512]{0:T(512)S(1)} %add_rsqrt_fusion, ...), kind=kOutput, calls=%fused_computation.38 | convolution fusion | flops 2474934272 | bytes 12775428 | tf_op jit(solution)/shard_map/dot_general | solution.py:39
  262.2 0.1 copy.13
  262.4 0.8 convert_element_type.129
  263.2 40.5 %all-reduce.9.cloned.1.call-done = (bf16[256,128]{1,0:T(8,128)(2,1)}, bf16[256,128]{1,0:T(8,128)(2,1)}, bf16[256,128]{1,0:T(8,128)(2,1)}) async-done(((bf16[256,128]{1,0:T(8,128)(2,1)}, bf16[256,128]{1,0:T(8,128)(2,1)}, bf16[256,128]{1,0:T(8,128)(2,1)}), (bf16[256,128]{1,0:T(8,128)(2,1)}, bf16[256,128]{1,0:T(8,128)(2,1)}, bf16[256,128]{1,0:T(8,128)(2,1)})) %all-reduce.9.cloned.1.call-update) | async-done | bytes 196624 | tf_op jit(solution)/shard_map/psum | solution.py:114
  303.7 1.5 abs_reduce_fusion
  305.2 37.2 %psum.46 = f32[]{:T(128)} all-reduce(f32[]{:T(128)} %abs_reduce_fusion), channel_id=1, replica_groups=mesh['mp'=4,'fsdp'=16,'dp'=4] {'fsdp'}, use_global_device_ids=true, to_apply=%region_11.12 | all-reduce | flops 1 | bytes 8 | tf_op jit(solution)/shard_map/psum | solution.py:124
  343.1 1.6 multiply_convert_fusion
  344.7 0.1 reshape.201
  344.8 8.2 %convolution_convert_fusion = bf16[3072,768]{1,0:T(8,128)(2,1)} fusion(bf16[512,64]{1,0:T(8,128)(2,1)S(1)} %reshape.201, bf16[3,64,768]{2,1,0:T(8,128)(2,1)S(1)} %copy-done.6, f32[512,3072]{1,0:T(8,128)} %copy-done, f32[3072]{0:T(1024)S(1)} %bitcast.104, f32[3072]{0:T(1024)S(1)} %bitcast.106, f32[512]{0:T(512)S(1)} %add_rsqrt_fusion.2, ...), kind=kOutput, calls=%fused_computation.7 | convolution fusion | flops 2476867584 | bytes 11268096 | tf_op jit(solution)/shard_map/dot_general | solution.py:133
  353.1 82.9 %reduce-scatter.2.cloned.1.call-done = bf16[192,768]{1,0:T(8,128)(2,1)} async-done(((bf16[3072,768]{1,0:T(8,128)(2,1)}), bf16[192,768]{1,0:T(8,128)(2,1)}) %reduce-scatter.2.cloned.1.call-update) | async-done | bytes 294928 | tf_op jit(solution)/shard_map/reduce_scatter | solution.py:132
  436.0 53.8 %all-reduce.7.cloned.1.call-done = bf16[192,768]{1,0:T(8,128)(2,1)} async-done(((bf16[192,768]{1,0:T(8,128)(2,1)}), bf16[192,768]{1,0:T(8,128)(2,1)}) %all-reduce.7.cloned.1.call-update) | async-done | bytes 294928 | tf_op jit(solution)/shard_map/psum | solution.py:140
  489.8 1.8 convert_element_type.139
  (36 shorter events, 0.6 us)
Async XLA Ops:
  7.2 65.3 %all-gather.7.cloned.1.call-start = ((), (), s32[]{:S(2)}) async-start(), calls=%async_computation.4 | async-start | bytes 5013504 | tf_op jit(solution)/shard_map/all_gather | solution.py:79
  9.3 112.0 %all-reduce.5.cloned.1.call-start = ((), (), s32[]{:S(2)}) async-start(), calls=%async_computation.1 | async-start | bytes 262144 | tf_op jit(solution)/shard_map/psum | solution.py:82
  41.7 30.8 %copy-start.6 = (bf16[3,64,768]{2,1,0:T(8,128)(2,1)S(1)}, bf16[3,64,768]{2,1,0:T(8,128)(2,1)}, u32[]{:S(2)}) copy-start(bf16[3,64,768]{2,1,0:T(8,128)(2,1)} %param.17) | copy-start | bytes 884740
  43.7 2.7 copy-start
  72.5 48.9 %copy-start.4 = (f32[1,256,128]{2,1,0:T(8,128)S(1)}, f32[1,256,128]{2,1,0:T(8,128)}, u32[]{:S(2)}) copy-start(f32[1,256,128]{2,1,0:T(8,128)} %param.10) | copy-start | bytes 393220
  72.5 49.9 %copy-start.3 = (bf16[3,64,3072]{2,1,0:T(8,128)(2,1)S(1)}, bf16[3,64,3072]{2,1,0:T(8,128)(2,1)}, u32[]{:S(2)}) copy-start(bf16[3,64,3072]{2,1,0:T(8,128)(2,1)} %param.14) | copy-start | bytes 3538948
  81.1 102.4 %all-gather.9.cloned.1.call-start = ((), (), s32[]{:S(2)}) async-start(), calls=%async_computation.5 | async-start | bytes 5013504 | tf_op jit(solution)/shard_map/all_gather | solution.py:94
  81.8 163.7 %all-gather.11.cloned.1.call-start = ((), (), s32[]{:S(2)}) async-start(), calls=%async_computation.6 | async-start | bytes 5013504 | tf_op jit(solution)/shard_map/all_gather | solution.py:93
  82.4 221.2 %all-reduce.9.cloned.1.call-start = ((), (), s32[]{:S(2)}) async-start(), calls=%async_computation.7 | async-start | bytes 393216 | tf_op jit(solution)/shard_map/psum | solution.py:114
  123.4 2.7 copy-start.2
  193.4 2.7 copy-start.1
  254.3 49.4 %copy-start.5 = (f32[256,128]{1,0:T(8,128)S(1)}, f32[256,128]{1,0:T(8,128)}, u32[]{:S(2)}) copy-start(f32[256,128]{1,0:T(8,128)} %all-reduce.5.cloned.1.call-done) | copy-start | bytes 393220
  263.1 172.8 %reduce-scatter.2.cloned.1.call-start = ((), (), s32[]{:S(2)}) async-start(), calls=%async_computation.2 | async-start | bytes 5013504 | tf_op jit(solution)/shard_map/reduce_scatter | solution.py:132
  353.0 136.8 %all-reduce.7.cloned.1.call-start = ((), (), s32[]{:S(2)}) async-start(), calls=%async_computation.3 | async-start | bytes 589824 | tf_op jit(solution)/shard_map/psum | solution.py:140
Sparse Core Ops, SparseCore 0:
  10.4 61.9 all-gather.6
  81.2 40.0 all-reduce.4
  124.1 59.4 all-gather.8
  186.7 58.7 all-gather.10
  263.3 40.3 all-reduce.8
  353.2 82.7 reduce-scatter.1
  438.6 51.1 all-reduce.6
where the time goes:
time: 499 us; the launch traced here: 498 us
  waiting for transfers between devices  348 us (70%)
  blocking collectives  60.9 us (12%)
  matrix products  49.3 us (10%)
  between operations  16.3 us (3%)
  local copies, waits for them, and re-layouts  13.7 us (3%)
  other arithmetic  10.1 us (2%)
    reduce_scatter x1, waiting for transfers between devices, body(): lax.psum_scatter(lax.dot_general(gen_hidden, upstream, (((0,), (0,)), (()...  82.9 us
    all_gather x1, waiting for transfers between devices, body(): lax.all_gather(proj_weight[2], 'fsdp', axis=0, tiled=True)  56.7 us
    psum x1, waiting for transfers between devices, body(): gen_grad = lax.psum(row_terms, 'dp').astype(jnp.float32)  53.8 us
    all_gather x1, waiting for transfers between devices, body(): lax.all_gather(proj_weight[1], 'fsdp', axis=0, tiled=True)  48.7 us
    psum x1, waiting for transfers between devices, body(): lax.psum(unembed_part(fake_cols + fake_part, unembed[2]).reshape(-1, 2 *...  40.5 us
    psum x1, waiting for transfers between devices, body(): clean_lat = lax.psum(clean_part, 'mp')  38.7 us
    psum x1, blocking collectives, body(): gap_total = lax.psum(jnp.sum(jnp.abs(clean_lat - real_pred)), 'fsdp')  37.2 us
    dot_general x4, matrix products, unembed_part(): lax.dot_general(residual_sum.astype(jnp.bfloat16), out_weight, (((1,), (1...  31.6 us
  transfers between devices with their start and end apart: 7, of which 7 were waited for; matrix products, arithmetic and copies ran while one was open for 5% of the time, Pallas kernels for 0%

commit v1 on v0

--- a/solution.py
+++ b/solution.py
@@ -70,7 +70,15 @@
         ],
         axis=0,
     )
-    modulation = lax.all_gather(local_mod, "fsdp", axis=1, tiled=True)
+    n = lax.axis_size("fsdp")
+    low = sorted(((dd, (dd + 1) % n) for dd in range(n)))
+    u_next = local_mod
+    slots = [u_next]
+    for dev in [*range(1, n)]:
+        u_next = lax.ppermute(u_next, axis_name="fsdp", perm=low)
+        slots.insert(0, u_next)
+    item_now = jnp.concatenate(slots, 1)
+    modulation = jnp.roll(item_now, (lax.axis_index("fsdp") + 1) * local_mod.shape[1], 1)
     latent = gen_noise[0].reshape(-1, CH)
     latent_bf = latent.astype(jnp.bfloat16)
     token_rows = latent.shape[0]

time: 499 us -> 547 us (1.096)
  waiting for transfers between devices: 348 us -> 419 us
  blocking collectives: 60.9 us -> 37.3 us
    ppermute x0 -> x15, waiting for transfers between devices: none -> 94.9 us  [body(): u_next = lax.ppermute(u_next, axis_name='fsdp', perm=low)]
    all_gather x1, waiting for transfers between devices: 25.2 us -> 0.02 us  [body(): lax.all_gather(proj_weight[0], 'fsdp', axis=0, tiled=True)]
    all_gather x1 -> x0, blocking collectives: 23.6 us -> none  [body(): modulation = lax.all_gather(local_mod, 'fsdp', axis=1, tiled=True)]
  transfers between devices with their start and end apart: 7 -> 22, of which waited for: 7 -> 21; matrix products, arithmetic and copies ran while one was open for 5% -> 4% of each run, Pallas kernels for 0% -> 0%
where the time goes in v1:
time: 547 us; the launch traced here: 546 us
  waiting for transfers between devices  419 us (77%)
  matrix products  49.2 us (9%)
  blocking collectives  37.3 us (7%)
  between operations  16.4 us (3%)
  local copies, waits for them, and re-layouts  11.3 us (2%)
  other arithmetic  10.3 us (2%)
    ppermute x15, waiting for transfers between devices, body(): u_next = lax.ppermute(u_next, axis_name='fsdp', perm=low)  94.9 us
    reduce_scatter x1, waiting for transfers between devices, body(): lax.psum_scatter(lax.dot_general(gen_hidden, upstream, (((0,), (0,)), (()...  82.7 us
    all_gather x1, waiting for transfers between devices, body(): lax.all_gather(proj_weight[2], 'fsdp', axis=0, tiled=True)  56.7 us
    psum x1, waiting for transfers between devices, body(): gen_grad = lax.psum(row_terms, 'dp').astype(jnp.float32)  53.8 us
    all_gather x1, waiting for transfers between devices, body(): lax.all_gather(proj_weight[1], 'fsdp', axis=0, tiled=True)  48.7 us
    psum x1, waiting for transfers between devices, body(): lax.psum(unembed_part(fake_cols + fake_part, unembed[2]).reshape(-1, 2 *...  40.5 us
    psum x1, waiting for transfers between devices, body(): clean_lat = lax.psum(clean_part, 'mp')  39.9 us
    psum x1, blocking collectives, body(): gap_total = lax.psum(jnp.sum(jnp.abs(clean_lat - real_pred)), 'fsdp')  37.3 us
  transfers between devices with their start and end apart: 22, of which 21 were waited for; matrix products, arithmetic and copies ran while one was open for 4% of the time, Pallas kernels for 0%

profile of v1, /device:TPU:2, one launch (start us, length us, event | category | flops | bytes accessed | tf_op | source)
XLA Modules:
  0.0 546.5 jit_solution(10075132419414955396)
XLA Ops:
  7.2 2.1 fusion.104
  11.6 1.3 fusion.49
  12.9 1.3 fusion.53
  14.2 1.3 fusion.51
  15.6 1.3 fusion.55
  17.0 1.6 collective-permute-start
  18.6 2.4 collective-permute-done
  21.0 1.2 collective-permute-start.1
  22.2 5.7 %collective-permute-done.1 = f32[4,384]{1,0:T(4,128)S(1)} collective-permute-done((f32[4,384]{1,0:T(4,128)S(1)}, f32[4,384]{1,0:T(4,128)S(1)}, u32[]{:S(2)}, u32[]{:S(2)}) %collective-permute-start.1) | collective-permute-done | bytes 6176 | tf_op jit(solution)/shard_map/ppermute | solution.py:78
  27.9 6.9 %collective-permute-done.2 = f32[4,384]{1,0:T(4,128)S(1)} collective-permute-done((f32[4,384]{1,0:T(4,128)S(1)}, f32[4,384]{1,0:T(4,128)S(1)}, u32[]{:S(2)}, u32[]{:S(2)}) %collective-permute-start.2) | collective-permute-done | bytes 6176 | tf_op jit(solution)/shard_map/ppermute | solution.py:78
  34.9 7.0 %collective-permute-done.3 = f32[4,384]{1,0:T(4,128)S(1)} collective-permute-done((f32[4,384]{1,0:T(4,128)S(1)}, f32[4,384]{1,0:T(4,128)S(1)}, u32[]{:S(2)}, u32[]{:S(2)}) %collective-permute-start.3) | collective-permute-done | bytes 6176 | tf_op jit(solution)/shard_map/ppermute | solution.py:78
  41.8 6.9 %collective-permute-done.4 = f32[4,384]{1,0:T(4,128)S(1)} collective-permute-done((f32[4,384]{1,0:T(4,128)S(1)}, f32[4,384]{1,0:T(4,128)S(1)}, u32[]{:S(2)}, u32[]{:S(2)}) %collective-permute-start.4) | collective-permute-done | bytes 6176 | tf_op jit(solution)/shard_map/ppermute | solution.py:78
  48.8 7.2 %collective-permute-done.5 = f32[4,384]{1,0:T(4,128)S(1)} collective-permute-done((f32[4,384]{1,0:T(4,128)S(1)}, f32[4,384]{1,0:T(4,128)S(1)}, u32[]{:S(2)}, u32[]{:S(2)}) %collective-permute-start.5) | collective-permute-done | bytes 6176 | tf_op jit(solution)/shard_map/ppermute | solution.py:78
  55.9 7.0 %collective-permute-done.6 = f32[4,384]{1,0:T(4,128)S(1)} collective-permute-done((f32[4,384]{1,0:T(4,128)S(1)}, f32[4,384]{1,0:T(4,128)S(1)}, u32[]{:S(2)}, u32[]{:S(2)}) %collective-permute-start.6) | collective-permute-done | bytes 6176 | tf_op jit(solution)/shard_map/ppermute | solution.py:78
  62.9 7.0 %collective-permute-done.7 = f32[4,384]{1,0:T(4,128)S(1)} collective-permute-done((f32[4,384]{1,0:T(4,128)S(1)}, f32[4,384]{1,0:T(4,128)S(1)}, u32[]{:S(2)}, u32[]{:S(2)}) %collective-permute-start.7) | collective-permute-done | bytes 6176 | tf_op jit(solution)/shard_map/ppermute | solution.py:78
  69.9 7.0 %collective-permute-done.8 = f32[4,384]{1,0:T(4,128)S(1)} collective-permute-done((f32[4,384]{1,0:T(4,128)S(1)}, f32[4,384]{1,0:T(4,128)S(1)}, u32[]{:S(2)}, u32[]{:S(2)}) %collective-permute-start.8) | collective-permute-done | bytes 6176 | tf_op jit(solution)/shard_map/ppermute | solution.py:78
  76.9 6.9 %collective-permute-done.9 = f32[4,384]{1,0:T(4,128)S(1)} collective-permute-done((f32[4,384]{1,0:T(4,128)S(1)}, f32[4,384]{1,0:T(4,128)S(1)}, u32[]{:S(2)}, u32[]{:S(2)}) %collective-permute-start.9) | collective-permute-done | bytes 6176 | tf_op jit(solution)/shard_map/ppermute | solution.py:78
  83.8 0.9 convert_element_type.109
  84.9 5.9 %collective-permute-done.10 = f32[4,384]{1,0:T(4,128)S(1)} collective-permute-done((f32[4,384]{1,0:T(4,128)S(1)}, f32[4,384]{1,0:T(4,128)S(1)}, u32[]{:S(2)}, u32[]{:S(2)}) %collective-permute-start.10) | collective-permute-done | bytes 6176 | tf_op jit(solution)/shard_map/ppermute | solution.py:78
  90.8 2.0 fusion.105
  92.8 4.9 collective-permute-done.11
  97.7 6.9 %collective-permute-done.12 = f32[4,384]{1,0:T(4,128)S(1)} collective-permute-done((f32[4,384]{1,0:T(4,128)S(1)}, f32[4,384]{1,0:T(4,128)S(1)}, u32[]{:S(2)}, u32[]{:S(2)}) %collective-permute-start.12) | collective-permute-done | bytes 6176 | tf_op jit(solution)/shard_map/ppermute | solution.py:78
  104.7 0.8 multiply_reduce_fusion.2
  105.4 6.2 %collective-permute-done.13 = f32[4,384]{1,0:T(4,128)S(1)} collective-permute-done((f32[4,384]{1,0:T(4,128)S(1)}, f32[4,384]{1,0:T(4,128)S(1)}, u32[]{:S(2)}, u32[]{:S(2)}) %collective-permute-start.13) | collective-permute-done | bytes 6176 | tf_op jit(solution)/shard_map/ppermute | solution.py:78
  111.6 6.9 %collective-permute-done.14 = f32[4,384]{1,0:T(4,128)S(1)} collective-permute-done((f32[4,384]{1,0:T(4,128)S(1)}, f32[4,384]{1,0:T(4,128)S(1)}, u32[]{:S(2)}, u32[]{:S(2)}) %collective-permute-start.14) | collective-permute-done | bytes 6176 | tf_op jit(solution)/shard_map/ppermute | solution.py:78
  119.3 7.9 %fusion.38 = f32[512,64]{1,0:T(8,128)S(1)} fusion(f32[512,3072]{1,0:T(8,128)} %copy-done, s32[]{:T(128)S(6)} %select_n.20, bf16[1,3072,768]{2,1,0:T(8,128)(2,1)} %all-gather.7.cloned.1.call-done, bf16[3,64,768]{2,1,0:T(8,128)(2,1)S(1)} %copy-done.6, f32[3072]{0:T(1024)S(1)} %bitcast.103, f32[3072]{0:T(1024)S(1)} %bitcast.105, f32[512]{0:T(512)S(1)} %add_rsqrt_fusion.2, ...), kind=kOutput, calls=%fused_computation.36 | convolution fusion | flops 2474901504 | bytes 12840964 | tf_op jit(solution)/shard_map/dot_general | solution.py:39
  127.2 0.8 reshape.200
  129.6 39.9 %all-reduce.5.cloned.1.call-done = f32[256,128]{1,0:T(8,128)} async-done(((f32[256,128]{1,0:T(8,128)}), f32[256,128]{1,0:T(8,128)}) %all-reduce.5.cloned.1.call-update) | async-done | bytes 131088 | tf_op jit(solution)/shard_map/psum | solution.py:90
  169.5 0.9 fusion.85
  170.5 1.0 fusion.106
  171.6 2.6 copy-done.2
  174.2 0.8 multiply_reduce_fusion.1
  175.0 56.7 %all-gather.9.cloned.1.call-done = bf16[1,3072,768]{2,1,0:T(8,128)(2,1)} async-done(((bf16[1,192,768]{2,1,0:T(8,128)(2,1)}), bf16[1,3072,768]{2,1,0:T(8,128)(2,1)}) %all-gather.9.cloned.1.call-update) | async-done | bytes 4718608 | tf_op jit(solution)/shard_map/all_gather | solution.py:102
  231.7 7.9 %fusion.46 = bf16[512,64]{0,1:T(8,128)(2,1)S(1)} fusion(f32[512,3072]{1,0:T(8,128)} %copy-done.2, s32[]{:T(128)S(6)} %select_n.20, bf16[1,3072,768]{2,1,0:T(8,128)(2,1)} %all-gather.9.cloned.1.call-done, f32[3072]{0:T(1024)S(1)} %bitcast.111, f32[3072]{0:T(1024)S(1)} %bitcast.112, f32[512]{0:T(512)S(1)} %add_rsqrt_fusion.1, ...), kind=kOutput, calls=%fused_computation.39 | convolution fusion | flops 2474934272 | bytes 12775428 | tf_op jit(solution)/shard_map/dot_general | solution.py:39
  240.5 1.0 fusion.107
  241.6 2.6 copy-done.1
  244.2 0.8 multiply_reduce_fusion
  245.0 48.7 %all-gather.11.cloned.1.call-done = bf16[1,3072,768]{2,1,0:T(8,128)(2,1)} async-done(((bf16[1,192,768]{2,1,0:T(8,128)(2,1)}), bf16[1,3072,768]{2,1,0:T(8,128)(2,1)}) %all-gather.11.cloned.1.call-update) | async-done | bytes 4718608 | tf_op jit(solution)/shard_map/all_gather | solution.py:101
  293.7 7.9 %fusion.40 = bf16[512,64]{0,1:T(8,128)(2,1)S(1)} fusion(f32[512,3072]{1,0:T(8,128)} %copy-done.1, s32[]{:T(128)S(6)} %select_n.20, bf16[1,3072,768]{2,1,0:T(8,128)(2,1)} %all-gather.11.cloned.1.call-done, f32[3072]{0:T(1024)S(1)} %bitcast.110, f32[3072]{0:T(1024)S(1)} %bitcast.109, f32[512]{0:T(512)S(1)} %add_rsqrt_fusion, ...), kind=kOutput, calls=%fused_computation.37 | convolution fusion | flops 2474934272 | bytes 12775428 | tf_op jit(solution)/shard_map/dot_general | solution.py:39
  302.4 7.9 %fusion.43 = bf16[512,64]{0,1:T(8,128)(2,1)S(1)} fusion(f32[512,3072]{1,0:T(8,128)} %copy-done.1, s32[]{:T(128)S(6)} %select_n.20, bf16[1,3072,768]{2,1,0:T(8,128)(2,1)} %all-gather.11.cloned.1.call-done, f32[3072]{0:T(1024)S(1)} %bitcast.108, f32[3072]{0:T(1024)S(1)} %bitcast.107, f32[512]{0:T(512)S(1)} %add_rsqrt_fusion, ...), kind=kOutput, calls=%fused_computation.38 | convolution fusion | flops 2474934272 | bytes 12775428 | tf_op jit(solution)/shard_map/dot_general | solution.py:39
  311.3 40.5 %all-reduce.9.cloned.1.call-done = (bf16[256,128]{1,0:T(8,128)(2,1)}, bf16[256,128]{1,0:T(8,128)(2,1)}, bf16[256,128]{1,0:T(8,128)(2,1)}) async-done(((bf16[256,128]{1,0:T(8,128)(2,1)}, bf16[256,128]{1,0:T(8,128)(2,1)}, bf16[256,128]{1,0:T(8,128)(2,1)}), (bf16[256,128]{1,0:T(8,128)(2,1)}, bf16[256,128]{1,0:T(8,128)(2,1)}, bf16[256,128]{1,0:T(8,128)(2,1)})) %all-reduce.9.cloned.1.call-update) | async-done | bytes 196624 | tf_op jit(solution)/shard_map/psum | solution.py:122
  351.8 1.5 abs_reduce_fusion
  353.3 37.3 %psum.46 = f32[]{:T(128)} all-reduce(f32[]{:T(128)} %abs_reduce_fusion), channel_id=1, replica_groups=mesh['mp'=4,'fsdp'=16,'dp'=4] {'fsdp'}, use_global_device_ids=true, to_apply=%region_11.12 | all-reduce | flops 1 | bytes 8 | tf_op jit(solution)/shard_map/psum | solution.py:132
  391.3 1.6 multiply_convert_fusion
  393.0 8.2 %convolution_convert_fusion = bf16[3072,768]{1,0:T(8,128)(2,1)} fusion(bf16[512,64]{1,0:T(8,128)(2,1)S(1)} %reshape.201, bf16[3,64,768]{2,1,0:T(8,128)(2,1)S(1)} %copy-done.6, f32[512,3072]{1,0:T(8,128)} %copy-done, f32[3072]{0:T(1024)S(1)} %bitcast.104, f32[3072]{0:T(1024)S(1)} %bitcast.106, f32[512]{0:T(512)S(1)} %add_rsqrt_fusion.2, ...), kind=kOutput, calls=%fused_computation.7 | convolution fusion | flops 2476867584 | bytes 11268096 | tf_op jit(solution)/shard_map/dot_general | solution.py:141
  401.3 82.7 %reduce-scatter.2.cloned.1.call-done = bf16[192,768]{1,0:T(8,128)(2,1)} async-done(((bf16[3072,768]{1,0:T(8,128)(2,1)}), bf16[192,768]{1,0:T(8,128)(2,1)}) %reduce-scatter.2.cloned.1.call-update) | async-done | bytes 294928 | tf_op jit(solution)/shard_map/reduce_scatter | solution.py:140
  484.0 53.8 %all-reduce.7.cloned.1.call-done = bf16[192,768]{1,0:T(8,128)(2,1)} async-done(((bf16[192,768]{1,0:T(8,128)(2,1)}), bf16[192,768]{1,0:T(8,128)(2,1)}) %all-reduce.7.cloned.1.call-update) | async-done | bytes 294928 | tf_op jit(solution)/shard_map/psum | solution.py:148
  537.8 1.8 convert_element_type.139
  (97 shorter events, 6.3 us)
Async XLA Ops:
  7.2 112.1 %all-gather.7.cloned.1.call-start = ((), (), s32[]{:S(2)}) async-start(), calls=%async_computation.4 | async-start | bytes 5013504 | tf_op jit(solution)/shard_map/all_gather | solution.py:87
  9.3 160.2 %all-reduce.5.cloned.1.call-start = ((), (), s32[]{:S(2)}) async-start(), calls=%async_computation.1 | async-start | bytes 262144 | tf_op jit(solution)/shard_map/psum | solution.py:90
  17.0 4.0 collective-permute-start
  21.0 6.9 %collective-permute-start.1 = (f32[4,384]{1,0:T(4,128)S(1)}, f32[4,384]{1,0:T(4,128)S(1)}, u32[]{:S(2)}, u32[]{:S(2)}) collective-permute-start(f32[4,384]{1,0:T(4,128)S(1)} %collective-permute-done), channel_id=1, source_target_pairs={{0,4},{4,8},{8,12},{12,16},{16,20},{20,24},{24,28},{28,32},{32,36}... | collective-permute-start | bytes 18440 | tf_op jit(solution)/shard_map/ppermute | solution.py:78
  27.9 6.9 %collective-permute-start.2 = (f32[4,384]{1,0:T(4,128)S(1)}, f32[4,384]{1,0:T(4,128)S(1)}, u32[]{:S(2)}, u32[]{:S(2)}) collective-permute-start(f32[4,384]{1,0:T(4,128)S(1)} %collective-permute-done.1), channel_id=1, source_target_pairs={{0,4},{4,8},{8,12},{12,16},{16,20},{20,24},{24,28},{28,32},{32,36}... | collective-permute-start | bytes 18440 | tf_op jit(solution)/shard_map/ppermute | solution.py:78
  34.8 7.0 %collective-permute-start.3 = (f32[4,384]{1,0:T(4,128)S(1)}, f32[4,384]{1,0:T(4,128)S(1)}, u32[]{:S(2)}, u32[]{:S(2)}) collective-permute-start(f32[4,384]{1,0:T(4,128)S(1)} %collective-permute-done.2), channel_id=1, source_target_pairs={{0,4},{4,8},{8,12},{12,16},{16,20},{20,24},{24,28},{28,32},{32,36}... | collective-permute-start | bytes 18440 | tf_op jit(solution)/shard_map/ppermute | solution.py:78
  41.8 7.0 %collective-permute-start.4 = (f32[4,384]{1,0:T(4,128)S(1)}, f32[4,384]{1,0:T(4,128)S(1)}, u32[]{:S(2)}, u32[]{:S(2)}) collective-permute-start(f32[4,384]{1,0:T(4,128)S(1)} %collective-permute-done.3), channel_id=1, source_target_pairs={{0,4},{4,8},{8,12},{12,16},{16,20},{20,24},{24,28},{28,32},{32,36}... | collective-permute-start | bytes 18440 | tf_op jit(solution)/shard_map/ppermute | solution.py:78
  48.8 7.2 %collective-permute-start.5 = (f32[4,384]{1,0:T(4,128)S(1)}, f32[4,384]{1,0:T(4,128)S(1)}, u32[]{:S(2)}, u32[]{:S(2)}) collective-permute-start(f32[4,384]{1,0:T(4,128)S(1)} %collective-permute-done.4), channel_id=1, source_target_pairs={{0,4},{4,8},{8,12},{12,16},{16,20},{20,24},{24,28},{28,32},{32,36}... | collective-permute-start | bytes 18440 | tf_op jit(solution)/shard_map/ppermute | solution.py:78
  55.9 7.0 %collective-permute-start.6 = (f32[4,384]{1,0:T(4,128)S(1)}, f32[4,384]{1,0:T(4,128)S(1)}, u32[]{:S(2)}, u32[]{:S(2)}) collective-permute-start(f32[4,384]{1,0:T(4,128)S(1)} %collective-permute-done.5), channel_id=1, source_target_pairs={{0,4},{4,8},{8,12},{12,16},{16,20},{20,24},{24,28},{28,32},{32,36}... | collective-permute-start | bytes 18440 | tf_op jit(solution)/shard_map/ppermute | solution.py:78
  62.9 7.0 %collective-permute-start.7 = (f32[4,384]{1,0:T(4,128)S(1)}, f32[4,384]{1,0:T(4,128)S(1)}, u32[]{:S(2)}, u32[]{:S(2)}) collective-permute-start(f32[4,384]{1,0:T(4,128)S(1)} %collective-permute-done.6), channel_id=1, source_target_pairs={{0,4},{4,8},{8,12},{12,16},{16,20},{20,24},{24,28},{28,32},{32,36}... | collective-permute-start | bytes 18440 | tf_op jit(solution)/shard_map/ppermute | solution.py:78
  69.9 7.0 %collective-permute-start.8 = (f32[4,384]{1,0:T(4,128)S(1)}, f32[4,384]{1,0:T(4,128)S(1)}, u32[]{:S(2)}, u32[]{:S(2)}) collective-permute-start(f32[4,384]{1,0:T(4,128)S(1)} %collective-permute-done.7), channel_id=1, source_target_pairs={{0,4},{4,8},{8,12},{12,16},{16,20},{20,24},{24,28},{28,32},{32,36}... | collective-permute-start | bytes 18440 | tf_op jit(solution)/shard_map/ppermute | solution.py:78
  76.9 6.9 %collective-permute-start.9 = (f32[4,384]{1,0:T(4,128)S(1)}, f32[4,384]{1,0:T(4,128)S(1)}, u32[]{:S(2)}, u32[]{:S(2)}) collective-permute-start(f32[4,384]{1,0:T(4,128)S(1)} %collective-permute-done.8), channel_id=1, source_target_pairs={{0,4},{4,8},{8,12},{12,16},{16,20},{20,24},{24,28},{28,32},{32,36}... | collective-permute-start | bytes 18440 | tf_op jit(solution)/shard_map/ppermute | solution.py:78
  83.8 6.9 %collective-permute-start.10 = (f32[4,384]{1,0:T(4,128)S(1)}, f32[4,384]{1,0:T(4,128)S(1)}, u32[]{:S(2)}, u32[]{:S(2)}) collective-permute-start(f32[4,384]{1,0:T(4,128)S(1)} %collective-permute-done.9), channel_id=1, source_target_pairs={{0,4},{4,8},{8,12},{12,16},{16,20},{20,24},{24,28},{28,32},{32,36}... | collective-permute-start | bytes 18440 | tf_op jit(solution)/shard_map/ppermute | solution.py:78
  84.9 34.4 %copy-start.6 = (bf16[3,64,768]{2,1,0:T(8,128)(2,1)S(1)}, bf16[3,64,768]{2,1,0:T(8,128)(2,1)}, u32[]{:S(2)}) copy-start(bf16[3,64,768]{2,1,0:T(8,128)(2,1)} %param.17) | copy-start | bytes 884740
  90.8 6.9 %collective-permute-start.11 = (f32[4,384]{1,0:T(4,128)S(1)}, f32[4,384]{1,0:T(4,128)S(1)}, u32[]{:S(2)}, u32[]{:S(2)}) collective-permute-start(f32[4,384]{1,0:T(4,128)S(1)} %collective-permute-done.10), channel_id=1, source_target_pairs={{0,4},{4,8},{8,12},{12,16},{16,20},{20,24},{24,28},{28,32},{32,36}... | collective-permute-start | bytes 18440 | tf_op jit(solution)/shard_map/ppermute | solution.py:78
  92.8 11.9 %copy-start = (f32[512,3072]{1,0:T(8,128)}, f32[512,3072]{1,0:T(8,128)S(1)}, u32[]{:S(2)}) copy-start(f32[512,3072]{1,0:T(8,128)S(1)} %get-tuple-element.22) | copy-start | bytes 18874372
  97.7 6.9 %collective-permute-start.12 = (f32[4,384]{1,0:T(4,128)S(1)}, f32[4,384]{1,0:T(4,128)S(1)}, u32[]{:S(2)}, u32[]{:S(2)}) collective-permute-start(f32[4,384]{1,0:T(4,128)S(1)} %collective-permute-done.11), channel_id=1, source_target_pairs={{0,4},{4,8},{8,12},{12,16},{16,20},{20,24},{24,28},{28,32},{32,36}... | collective-permute-start | bytes 18440 | tf_op jit(solution)/shard_map/ppermute | solution.py:78
  104.7 7.0 %collective-permute-start.13 = (f32[4,384]{1,0:T(4,128)S(1)}, f32[4,384]{1,0:T(4,128)S(1)}, u32[]{:S(2)}, u32[]{:S(2)}) collective-permute-start(f32[4,384]{1,0:T(4,128)S(1)} %collective-permute-done.12), channel_id=1, source_target_pairs={{0,4},{4,8},{8,12},{12,16},{16,20},{20,24},{24,28},{28,32},{32,36}... | collective-permute-start | bytes 18440 | tf_op jit(solution)/shard_map/ppermute | solution.py:78
  111.6 6.9 %collective-permute-start.14 = (f32[4,384]{1,0:T(4,128)S(1)}, f32[4,384]{1,0:T(4,128)S(1)}, u32[]{:S(2)}, u32[]{:S(2)}) collective-permute-start(f32[4,384]{1,0:T(4,128)S(1)} %collective-permute-done.13), channel_id=1, source_target_pairs={{0,4},{4,8},{8,12},{12,16},{16,20},{20,24},{24,28},{28,32},{32,36}... | collective-permute-start | bytes 18440 | tf_op jit(solution)/shard_map/ppermute | solution.py:78
  119.3 50.2 %copy-start.4 = (f32[1,256,128]{2,1,0:T(8,128)S(1)}, f32[1,256,128]{2,1,0:T(8,128)}, u32[]{:S(2)}) copy-start(f32[1,256,128]{2,1,0:T(8,128)} %param.10) | copy-start | bytes 393220
  119.3 51.2 %copy-start.3 = (bf16[3,64,3072]{2,1,0:T(8,128)(2,1)S(1)}, bf16[3,64,3072]{2,1,0:T(8,128)(2,1)}, u32[]{:S(2)}) copy-start(bf16[3,64,3072]{2,1,0:T(8,128)(2,1)} %param.14) | copy-start | bytes 3538948
  128.0 103.7 %all-gather.9.cloned.1.call-start = ((), (), s32[]{:S(2)}) async-start(), calls=%async_computation.5 | async-start | bytes 5013504 | tf_op jit(solution)/shard_map/all_gather | solution.py:102
  128.7 165.0 %all-gather.11.cloned.1.call-start = ((), (), s32[]{:S(2)}) async-start(), calls=%async_computation.6 | async-start | bytes 5013504 | tf_op jit(solution)/shard_map/all_gather | solution.py:101
  129.3 222.5 %all-reduce.9.cloned.1.call-start = ((), (), s32[]{:S(2)}) async-start(), calls=%async_computation.7 | async-start | bytes 393216 | tf_op jit(solution)/shard_map/psum | solution.py:122
  171.6 2.6 copy-start.2
  241.5 2.6 copy-start.1
  302.4 49.4 %copy-start.5 = (f32[256,128]{1,0:T(8,128)S(1)}, f32[256,128]{1,0:T(8,128)}, u32[]{:S(2)}) copy-start(f32[256,128]{1,0:T(8,128)} %all-reduce.5.cloned.1.call-done) | copy-start | bytes 393220
  311.3 172.7 %reduce-scatter.2.cloned.1.call-start = ((), (), s32[]{:S(2)}) async-start(), calls=%async_computation.2 | async-start | bytes 5013504 | tf_op jit(solution)/shard_map/reduce_scatter | solution.py:140
  401.2 136.6 %all-reduce.7.cloned.1.call-start = ((), (), s32[]{:S(2)}) async-start(), calls=%async_computation.3 | async-start | bytes 589824 | tf_op jit(solution)/shard_map/psum | solution.py:148
Sparse Core Ops, SparseCore 0:
  10.4 61.9 all-gather.6
  128.1 41.3 all-reduce.4
  172.2 59.4 all-gather.8
  234.9 58.7 all-gather.10
  311.4 40.3 all-reduce.8
  401.3 82.5 reduce-scatter.1
  486.6 51.1 all-reduce.6
